TPU v7x, 32 devices: a whole 2x2x4 slice. The times are simulated.
32 devices in a mesh: sec: 4 (over x, core), row: 8 (over z, y).
Axes of the slice: x: 2, y: 2, z: 4, core: 2. Of those that a mesh axis runs over, the one named last changes fastest.
Arguments:
- factor: float32 [4, 2048, 8192], P(None, 'row', 'sec'), may hold values from -0.0625 to 0.0625
- inverse_blocks: float32 [4, 2048, 2048], P('sec', 'row'), may hold values from -4 to 4, as said below
- right_side: float32 [4, 2048, 384], P('sec', 'row'), may hold values from -6 to 6
Outputs:
- solution: float32 [4, 2048, 384], P('sec', 'row')
Inputs may be any that keep to these rules, and one draw needn't show every extreme that they name: `inverse_blocks`: each block is nonsingular; it stands for the inverse of the factor's diagonal block of that section.
All inputs are finite; a program needn't handle non-finite values.
Results may differ from a plain program's by a relative error of at most 0.0001.
Values sent between devices are 32-bit elements; how exact they have to be, the bound alone decides.
A program may use at most 64 MiB of HBM per device.

v0:
```python
import jax
import jax.numpy as jnp
from jax import lax
from jax.sharding import PartitionSpec as P

MICRO = 3
WIDTH = 128
highest = lax.Precision.HIGHEST


def passed_along(block, axis, distance):
    devices = range(lax.axis_size(axis))
    route = [(i - distance, i) for i in devices if i - distance in devices]
    return lax.ppermute(block, axis, route)


def shards(factor, inverse_blocks, right_side):
    sections = lax.axis_size("sec")
    segment = lax.axis_index("sec")
    local_rows = factor.shape[1]
    block_cols = factor.shape[2]
    width = WIDTH
    own_inverse = inverse_blocks[0]
    panel_rows = factor.reshape(sections * local_rows, block_cols)

    def fold_update(carry, piece):
        return carry + jnp.dot(panel_rows, piece, precision=highest)

    def advance(tick_index, state):
        carried, head, solution = state
        group = tick_index - segment
        valid = jnp.logical_and(group >= 0, group < MICRO)
        clipped = jnp.clip(group, 0, MICRO - 1)
        start_col = clipped * width
        own_rhs = lax.dynamic_slice_in_dim(right_side[0], start_col, width, 1)
        own_sum = head
        residual = own_rhs - own_sum
        full_residual = lax.all_gather(residual, "row", axis=0, tiled=True)
        own_result = jnp.dot(own_inverse, full_residual, precision=highest)
        updated = lax.dynamic_update_slice_in_dim(solution, own_result, start_col, 1)
        solution = jnp.where(valid, updated, solution)
        flat_in = carried.reshape(sections * local_rows, width)
        outgoing = fold_update(flat_in, lax.all_gather(own_result, "row", axis=0, tiled=True))
        outgoing = outgoing.reshape(sections, local_rows, width)
        following = jnp.minimum(segment + 1, sections - 1)
        next_sum = lax.dynamic_index_in_dim(outgoing, following, 0, keepdims=False)
        head = passed_along(next_sum, "sec", 1)
        carried = passed_along(outgoing, "sec", 1)
        return (carried, head, solution)

    initial = (
        jnp.zeros((sections, local_rows, width), jnp.float32),
        jnp.zeros((local_rows, width), jnp.float32),
        jnp.zeros(right_side.shape[1:], jnp.float32),
    )
    final = lax.fori_loop(0, sections + MICRO - 1, advance, initial)
    return final[2][None]


def solution(mesh):
    return jax.shard_map(
        shards,
        mesh=mesh,
        in_specs=(P(None, "row", "sec"), P("sec", "row", None), P("sec", "row", None)),
        out_specs=P("sec", "row", None),
        check_vma=False,
    )
```

profile of v0, /device:TPU:1, one launch (start us, length us, event | category | flops | bytes accessed | tf_op | source)
XLA Modules:
  0.0 665.9 jit_solution(2073231575732520902)
XLA Ops:
  6.7 651.6 %while.19 = (s32[]{:T(128)}, f32[4,256,128]{1,0,2:T(4,128)S(1)}, f32[256,128]{0,1:T(8,128)S(1)}, f32[256,384]{1,0:T(8,128)S(1)}, s32[]{:T(128)}, /*index=5*/f32[...) while((s32[]{:T(128)}, f32[4,256,128]{1,0,2:T(4,128)S(1)}, ...), condition=%wide.region_1.2_spmd, body=%wide.region_0.1_spmd.sunk | while | flops 4026728448 | bytes 28311972 | solution.py:56
  8.7 39.9 %all-gather.3.cloned.1.call-done = f32[2048,128]{0,1:T(8,128)} async-done(((f32[256,128]{0,1:T(8,128)}), f32[2048,128]{0,1:T(8,128)}) %all-gather.3.cloned.1.call-update) | async-done | bytes 1048592 | tf_op jit(solution)/shard_map/while/body/eval_jaxpr/all_gather | solution.py:38
  53.5 38.5 %all-gather.5.cloned.1.call-done = f32[2048,128]{0,1:T(8,128)} async-done(((f32[256,128]{0,1:T(8,128)}), f32[2048,128]{0,1:T(8,128)}) %all-gather.5.cloned.1.call-update) | async-done | bytes 1048592 | tf_op jit(solution)/shard_map/while/body/eval_jaxpr/all_gather | solution.py:43
  91.9 11.4 %fusion.14 = f32[1024,128]{0,1:T(8,128)S(1)} fusion(f32[1024,128]{0,1:T(8,128)S(1)} %bitcast.43, f32[2048,128]{0,1:T(8,128)} %all-gather.5.cloned.1.call-done, f32[1024,2048]{1,0:T(8,128)} %get-tuple-element.330), kind=kOutput, calls=%fused_computation.1.clone.1 | convolution fusion | flops 3221356544 | bytes 10485760 | tf_op jit(solution)/shard_map/while/body/eval_jaxpr/dot_general | solution.py:27
  119.3 37.5 %all-gather.3.cloned.1.call-done = f32[2048,128]{0,1:T(8,128)} async-done(((f32[256,128]{0,1:T(8,128)}), f32[2048,128]{0,1:T(8,128)}) %all-gather.3.cloned.1.call-update) | async-done | bytes 1048592 | tf_op jit(solution)/shard_map/while/body/eval_jaxpr/all_gather | solution.py:38
  161.7 38.5 %all-gather.5.cloned.1.call-done = f32[2048,128]{0,1:T(8,128)} async-done(((f32[256,128]{0,1:T(8,128)}), f32[2048,128]{0,1:T(8,128)}) %all-gather.5.cloned.1.call-update) | async-done | bytes 1048592 | tf_op jit(solution)/shard_map/while/body/eval_jaxpr/all_gather | solution.py:43
  200.2 11.4 %fusion.14 = f32[1024,128]{0,1:T(8,128)S(1)} fusion(f32[1024,128]{0,1:T(8,128)S(1)} %bitcast.43, f32[2048,128]{0,1:T(8,128)} %all-gather.5.cloned.1.call-done, f32[1024,2048]{1,0:T(8,128)} %get-tuple-element.330), kind=kOutput, calls=%fused_computation.1.clone.1 | convolution fusion | flops 3221356544 | bytes 10485760 | tf_op jit(solution)/shard_map/while/body/eval_jaxpr/dot_general | solution.py:27
  211.8 6.3 collective-permute-start
  227.5 37.2 %all-gather.3.cloned.1.call-done = f32[2048,128]{0,1:T(8,128)} async-done(((f32[256,128]{0,1:T(8,128)}), f32[2048,128]{0,1:T(8,128)}) %all-gather.3.cloned.1.call-update) | async-done | bytes 1048592 | tf_op jit(solution)/shard_map/while/body/eval_jaxpr/all_gather | solution.py:38
  269.6 38.5 %all-gather.5.cloned.1.call-done = f32[2048,128]{0,1:T(8,128)} async-done(((f32[256,128]{0,1:T(8,128)}), f32[2048,128]{0,1:T(8,128)}) %all-gather.5.cloned.1.call-update) | async-done | bytes 1048592 | tf_op jit(solution)/shard_map/while/body/eval_jaxpr/all_gather | solution.py:43
  308.1 11.4 %fusion.14 = f32[1024,128]{0,1:T(8,128)S(1)} fusion(f32[1024,128]{0,1:T(8,128)S(1)} %bitcast.43, f32[2048,128]{0,1:T(8,128)} %all-gather.5.cloned.1.call-done, f32[1024,2048]{1,0:T(8,128)} %get-tuple-element.330), kind=kOutput, calls=%fused_computation.1.clone.1 | convolution fusion | flops 3221356544 | bytes 10485760 | tf_op jit(solution)/shard_map/while/body/eval_jaxpr/dot_general | solution.py:27
  319.8 6.3 collective-permute-start
  335.5 37.5 %all-gather.3.cloned.1.call-done = f32[2048,128]{0,1:T(8,128)} async-done(((f32[256,128]{0,1:T(8,128)}), f32[2048,128]{0,1:T(8,128)}) %all-gather.3.cloned.1.call-update) | async-done | bytes 1048592 | tf_op jit(solution)/shard_map/while/body/eval_jaxpr/all_gather | solution.py:38
  377.9 38.5 %all-gather.5.cloned.1.call-done = f32[2048,128]{0,1:T(8,128)} async-done(((f32[256,128]{0,1:T(8,128)}), f32[2048,128]{0,1:T(8,128)}) %all-gather.5.cloned.1.call-update) | async-done | bytes 1048592 | tf_op jit(solution)/shard_map/while/body/eval_jaxpr/all_gather | solution.py:43
  416.4 11.4 %fusion.14 = f32[1024,128]{0,1:T(8,128)S(1)} fusion(f32[1024,128]{0,1:T(8,128)S(1)} %bitcast.43, f32[2048,128]{0,1:T(8,128)} %all-gather.5.cloned.1.call-done, f32[1024,2048]{1,0:T(8,128)} %get-tuple-element.330), kind=kOutput, calls=%fused_computation.1.clone.1 | convolution fusion | flops 3221356544 | bytes 10485760 | tf_op jit(solution)/shard_map/while/body/eval_jaxpr/dot_general | solution.py:27
  428.0 6.3 collective-permute-start
  443.7 37.5 %all-gather.3.cloned.1.call-done = f32[2048,128]{0,1:T(8,128)} async-done(((f32[256,128]{0,1:T(8,128)}), f32[2048,128]{0,1:T(8,128)}) %all-gather.3.cloned.1.call-update) | async-done | bytes 1048592 | tf_op jit(solution)/shard_map/while/body/eval_jaxpr/all_gather | solution.py:38
  486.1 38.5 %all-gather.5.cloned.1.call-done = f32[2048,128]{0,1:T(8,128)} async-done(((f32[256,128]{0,1:T(8,128)}), f32[2048,128]{0,1:T(8,128)}) %all-gather.5.cloned.1.call-update) | async-done | bytes 1048592 | tf_op jit(solution)/shard_map/while/body/eval_jaxpr/all_gather | solution.py:43
  524.6 11.4 %fusion.14 = f32[1024,128]{0,1:T(8,128)S(1)} fusion(f32[1024,128]{0,1:T(8,128)S(1)} %bitcast.43, f32[2048,128]{0,1:T(8,128)} %all-gather.5.cloned.1.call-done, f32[1024,2048]{1,0:T(8,128)} %get-tuple-element.330), kind=kOutput, calls=%fused_computation.1.clone.1 | convolution fusion | flops 3221356544 | bytes 10485760 | tf_op jit(solution)/shard_map/while/body/eval_jaxpr/dot_general | solution.py:27
  536.3 6.3 collective-permute-start
  551.9 37.5 %all-gather.3.cloned.1.call-done = f32[2048,128]{0,1:T(8,128)} async-done(((f32[256,128]{0,1:T(8,128)}), f32[2048,128]{0,1:T(8,128)}) %all-gather.3.cloned.1.call-update) | async-done | bytes 1048592 | tf_op jit(solution)/shard_map/while/body/eval_jaxpr/all_gather | solution.py:38
  594.4 38.5 %all-gather.5.cloned.1.call-done = f32[2048,128]{0,1:T(8,128)} async-done(((f32[256,128]{0,1:T(8,128)}), f32[2048,128]{0,1:T(8,128)}) %all-gather.5.cloned.1.call-update) | async-done | bytes 1048592 | tf_op jit(solution)/shard_map/while/body/eval_jaxpr/all_gather | solution.py:43
  632.8 11.4 %fusion.14 = f32[1024,128]{0,1:T(8,128)S(1)} fusion(f32[1024,128]{0,1:T(8,128)S(1)} %bitcast.43, f32[2048,128]{0,1:T(8,128)} %all-gather.5.cloned.1.call-done, f32[1024,2048]{1,0:T(8,128)} %get-tuple-element.330), kind=kOutput, calls=%fused_computation.1.clone.1 | convolution fusion | flops 3221356544 | bytes 10485760 | tf_op jit(solution)/shard_map/while/body/eval_jaxpr/dot_general | solution.py:27
  644.5 6.3 collective-permute-start
  (120 shorter events, 94.0 us)
Async XLA Ops:
  6.7 41.9 %all-gather.3.cloned.1.call-start = ((), (), s32[]{:S(2)}) async-start(), calls=%async_computation | async-start | bytes 1179648 | tf_op jit(solution)/shard_map/while/body/eval_jaxpr/all_gather | solution.py:38
  8.5 83.5 %all-gather.5.cloned.1.call-start = ((), (), s32[]{:S(2)}) async-start(), calls=%async_computation.1 | async-start | bytes 1179648 | tf_op jit(solution)/shard_map/while/body/eval_jaxpr/all_gather | solution.py:43
  103.6 13.8 %collective-permute-start = (f32[4,256,128]{1,0,2:T(4,128)S(1)}, f32[4,256,128]{1,0,2:T(4,128)S(1)}, u32[]{:S(2)}, u32[]{:S(2)}) collective-permute-start(f32[4,256,128]{1,0,2:T(4,128)S(1)} %reshape.28), channel_id=1, source_target_pairs={{0,8},{8,16},{16,24},{1,9},{9,17},{17,25},{2,10},{10,18},{18,26},{... | collective-permute-start | bytes 1572872 | tf_op jit(solution)/shard_map/while/body/eval_jaxpr/ppermute | solution.py:14
  110.0 7.4 %collective-permute-start.1 = (f32[256,128]{0,1:T(8,128)S(1)}, f32[256,128]{0,1:T(8,128)S(1)}, u32[]{:S(2)}, u32[]{:S(2)}) collective-permute-start(f32[256,128]{0,1:T(8,128)S(1)} %bitcast.46), channel_id=1, source_target_pairs={{0,8},{8,16},{16,24},{1,9},{9,17},{17,25},{2,10},{10,18},{18,26},{... | collective-permute-start | bytes 393224 | tf_op jit(solution)/shard_map/while/body/eval_jaxpr/ppermute | solution.py:14
  117.4 39.4 %all-gather.3.cloned.1.call-start = ((), (), s32[]{:S(2)}) async-start(), calls=%async_computation | async-start | bytes 1179648 | tf_op jit(solution)/shard_map/while/body/eval_jaxpr/all_gather | solution.py:38
  119.1 81.1 %all-gather.5.cloned.1.call-start = ((), (), s32[]{:S(2)}) async-start(), calls=%async_computation.1 | async-start | bytes 1179648 | tf_op jit(solution)/shard_map/while/body/eval_jaxpr/all_gather | solution.py:43
  211.8 13.8 %collective-permute-start = (f32[4,256,128]{1,0,2:T(4,128)S(1)}, f32[4,256,128]{1,0,2:T(4,128)S(1)}, u32[]{:S(2)}, u32[]{:S(2)}) collective-permute-start(f32[4,256,128]{1,0,2:T(4,128)S(1)} %reshape.28), channel_id=1, source_target_pairs={{0,8},{8,16},{16,24},{1,9},{9,17},{17,25},{2,10},{10,18},{18,26},{... | collective-permute-start | bytes 1572872 | tf_op jit(solution)/shard_map/while/body/eval_jaxpr/ppermute | solution.py:14
  218.2 7.4 %collective-permute-start.1 = (f32[256,128]{0,1:T(8,128)S(1)}, f32[256,128]{0,1:T(8,128)S(1)}, u32[]{:S(2)}, u32[]{:S(2)}) collective-permute-start(f32[256,128]{0,1:T(8,128)S(1)} %bitcast.46), channel_id=1, source_target_pairs={{0,8},{8,16},{16,24},{1,9},{9,17},{17,25},{2,10},{10,18},{18,26},{... | collective-permute-start | bytes 393224 | tf_op jit(solution)/shard_map/while/body/eval_jaxpr/ppermute | solution.py:14
  225.6 39.1 %all-gather.3.cloned.1.call-start = ((), (), s32[]{:S(2)}) async-start(), calls=%async_computation | async-start | bytes 1179648 | tf_op jit(solution)/shard_map/while/body/eval_jaxpr/all_gather | solution.py:38
  227.3 80.8 %all-gather.5.cloned.1.call-start = ((), (), s32[]{:S(2)}) async-start(), calls=%async_computation.1 | async-start | bytes 1179648 | tf_op jit(solution)/shard_map/while/body/eval_jaxpr/all_gather | solution.py:43
  319.8 13.8 %collective-permute-start = (f32[4,256,128]{1,0,2:T(4,128)S(1)}, f32[4,256,128]{1,0,2:T(4,128)S(1)}, u32[]{:S(2)}, u32[]{:S(2)}) collective-permute-start(f32[4,256,128]{1,0,2:T(4,128)S(1)} %reshape.28), channel_id=1, source_target_pairs={{0,8},{8,16},{16,24},{1,9},{9,17},{17,25},{2,10},{10,18},{18,26},{... | collective-permute-start | bytes 1572872 | tf_op jit(solution)/shard_map/while/body/eval_jaxpr/ppermute | solution.py:14
  326.2 7.4 %collective-permute-start.1 = (f32[256,128]{0,1:T(8,128)S(1)}, f32[256,128]{0,1:T(8,128)S(1)}, u32[]{:S(2)}, u32[]{:S(2)}) collective-permute-start(f32[256,128]{0,1:T(8,128)S(1)} %bitcast.46), channel_id=1, source_target_pairs={{0,8},{8,16},{16,24},{1,9},{9,17},{17,25},{2,10},{10,18},{18,26},{... | collective-permute-start | bytes 393224 | tf_op jit(solution)/shard_map/while/body/eval_jaxpr/ppermute | solution.py:14
  333.5 39.4 %all-gather.3.cloned.1.call-start = ((), (), s32[]{:S(2)}) async-start(), calls=%async_computation | async-start | bytes 1179648 | tf_op jit(solution)/shard_map/while/body/eval_jaxpr/all_gather | solution.py:38
  335.3 81.1 %all-gather.5.cloned.1.call-start = ((), (), s32[]{:S(2)}) async-start(), calls=%async_computation.1 | async-start | bytes 1179648 | tf_op jit(solution)/shard_map/while/body/eval_jaxpr/all_gather | solution.py:43
  428.0 13.8 %collective-permute-start = (f32[4,256,128]{1,0,2:T(4,128)S(1)}, f32[4,256,128]{1,0,2:T(4,128)S(1)}, u32[]{:S(2)}, u32[]{:S(2)}) collective-permute-start(f32[4,256,128]{1,0,2:T(4,128)S(1)} %reshape.28), channel_id=1, source_target_pairs={{0,8},{8,16},{16,24},{1,9},{9,17},{17,25},{2,10},{10,18},{18,26},{... | collective-permute-start | bytes 1572872 | tf_op jit(solution)/shard_map/while/body/eval_jaxpr/ppermute | solution.py:14
  434.4 7.4 %collective-permute-start.1 = (f32[256,128]{0,1:T(8,128)S(1)}, f32[256,128]{0,1:T(8,128)S(1)}, u32[]{:S(2)}, u32[]{:S(2)}) collective-permute-start(f32[256,128]{0,1:T(8,128)S(1)} %bitcast.46), channel_id=1, source_target_pairs={{0,8},{8,16},{16,24},{1,9},{9,17},{17,25},{2,10},{10,18},{18,26},{... | collective-permute-start | bytes 393224 | tf_op jit(solution)/shard_map/while/body/eval_jaxpr/ppermute | solution.py:14
  441.8 39.4 %all-gather.3.cloned.1.call-start = ((), (), s32[]{:S(2)}) async-start(), calls=%async_computation | async-start | bytes 1179648 | tf_op jit(solution)/shard_map/while/body/eval_jaxpr/all_gather | solution.py:38
  443.5 81.1 %all-gather.5.cloned.1.call-start = ((), (), s32[]{:S(2)}) async-start(), calls=%async_computation.1 | async-start | bytes 1179648 | tf_op jit(solution)/shard_map/while/body/eval_jaxpr/all_gather | solution.py:43
  536.3 13.8 %collective-permute-start = (f32[4,256,128]{1,0,2:T(4,128)S(1)}, f32[4,256,128]{1,0,2:T(4,128)S(1)}, u32[]{:S(2)}, u32[]{:S(2)}) collective-permute-start(f32[4,256,128]{1,0,2:T(4,128)S(1)} %reshape.28), channel_id=1, source_target_pairs={{0,8},{8,16},{16,24},{1,9},{9,17},{17,25},{2,10},{10,18},{18,26},{... | collective-permute-start | bytes 1572872 | tf_op jit(solution)/shard_map/while/body/eval_jaxpr/ppermute | solution.py:14
  542.7 7.4 %collective-permute-start.1 = (f32[256,128]{0,1:T(8,128)S(1)}, f32[256,128]{0,1:T(8,128)S(1)}, u32[]{:S(2)}, u32[]{:S(2)}) collective-permute-start(f32[256,128]{0,1:T(8,128)S(1)} %bitcast.46), channel_id=1, source_target_pairs={{0,8},{8,16},{16,24},{1,9},{9,17},{17,25},{2,10},{10,18},{18,26},{... | collective-permute-start | bytes 393224 | tf_op jit(solution)/shard_map/while/body/eval_jaxpr/ppermute | solution.py:14
  550.0 39.4 %all-gather.3.cloned.1.call-start = ((), (), s32[]{:S(2)}) async-start(), calls=%async_computation | async-start | bytes 1179648 | tf_op jit(solution)/shard_map/while/body/eval_jaxpr/all_gather | solution.py:38
  551.8 81.1 %all-gather.5.cloned.1.call-start = ((), (), s32[]{:S(2)}) async-start(), calls=%async_computation.1 | async-start | bytes 1179648 | tf_op jit(solution)/shard_map/while/body/eval_jaxpr/all_gather | solution.py:43
  644.5 13.8 %collective-permute-start = (f32[4,256,128]{1,0,2:T(4,128)S(1)}, f32[4,256,128]{1,0,2:T(4,128)S(1)}, u32[]{:S(2)}, u32[]{:S(2)}) collective-permute-start(f32[4,256,128]{1,0,2:T(4,128)S(1)} %reshape.28), channel_id=1, source_target_pairs={{0,8},{8,16},{16,24},{1,9},{9,17},{17,25},{2,10},{10,18},{18,26},{... | collective-permute-start | bytes 1572872 | tf_op jit(solution)/shard_map/while/body/eval_jaxpr/ppermute | solution.py:14
  650.9 7.4 %collective-permute-start.1 = (f32[256,128]{0,1:T(8,128)S(1)}, f32[256,128]{0,1:T(8,128)S(1)}, u32[]{:S(2)}, u32[]{:S(2)}) collective-permute-start(f32[256,128]{0,1:T(8,128)S(1)} %bitcast.46), channel_id=1, source_target_pairs={{0,8},{8,16},{16,24},{1,9},{9,17},{17,25},{2,10},{10,18},{18,26},{... | collective-permute-start | bytes 393224 | tf_op jit(solution)/shard_map/while/body/eval_jaxpr/ppermute | solution.py:14
  (1 other events, 0.7 us)
Sparse Core Ops, SparseCore 0:
  9.5 38.9 all-gather.2
  53.5 38.3 all-gather.4
  120.2 36.5 all-gather.2
  161.7 38.4 all-gather.4
  228.1 36.5 all-gather.2
  269.7 38.3 all-gather.4
  336.4 36.5 all-gather.2
  377.9 38.4 all-gather.4
  444.6 36.5 all-gather.2
  486.1 38.4 all-gather.4
  552.9 36.5 all-gather.2
  594.4 38.4 all-gather.4
where the time goes:
time: 666 us
  waiting for transfers between devices  490 us (74%)
  matrix products  97.2 us (15%)
  starting transfers between devices  49.3 us (7%)
  between operations  13.4 us (2%)
  local copies, waits for them, and re-layouts  11.1 us (2%)
    all_gather x6, waiting for transfers between devices, advance(): lax.all_gather(own_result, 'row', axis=0, tiled=True)  231 us
    all_gather x6, waiting for transfers between devices, advance(): full_residual = lax.all_gather(residual, 'row', axis=0, tiled=True)  227 us
    dot_general x6, matrix products, fold_update(): return carry + jnp.dot(panel_rows, piece, precision=highest)  68.4 us
    ppermute x12, starting transfers between devices, passed_along(): return lax.ppermute(block, axis, route)  49 us
    ppermute x12, waiting for transfers between devices, passed_along(): return lax.ppermute(block, axis, route)  31.9 us
    dot_general x6, matrix products, advance(): own_result = jnp.dot(own_inverse, full_residual, precision=highest)  28.7 us
  transfers between devices with their start and end apart: 24, of which 18 were waited for; matrix products, arithmetic and copies ran while one was open for 0% of the time, Pallas kernels for 0%

commit v1 on v0

--- a/solution.py
+++ b/solution.py
@@ -35,7 +35,14 @@
         own_rhs = lax.dynamic_slice_in_dim(right_side[0], start_col, width, 1)
         own_sum = head
         residual = own_rhs - own_sum
-        full_residual = lax.all_gather(residual, "row", axis=0, tiled=True)
+        ring = [residual]
+        for hop in range(7):
+            ring.append(lax.ppermute(ring[-1], "row", [(dev, (dev + 1) % 8) for dev in range(8)]))
+        full_residual = jnp.roll(
+            jnp.concatenate(ring[::-1], axis=0),
+            (lax.axis_index("row") + 1) * ring[0].shape[0],
+            axis=0,
+        )
         own_result = jnp.dot(own_inverse, full_residual, precision=highest)
         updated = lax.dynamic_update_slice_in_dim(solution, own_result, start_col, 1)
         solution = jnp.where(valid, updated, solution)

time: 666 us -> 749 us (1.12)
  waiting for transfers between devices: 490 us -> 550 us
  local copies, waits for them, and re-layouts: 11.1 us -> 37 us
  matrix products: 97.2 us -> 85.6 us
    ppermute x0 -> x42, waiting for transfers between devices: none -> 274 us  [advance(): lax.ppermute(ring[-1], 'row', [(dev, (dev + 1) % 8) for dev in range(8)])]
    all_gather x6 -> x0, waiting for transfers between devices: 227 us -> none  [advance(): full_residual = lax.all_gather(residual, 'row', axis=0, tiled=True)]
    all_gather x6, waiting for transfers between devices: 231 us -> 249 us  [advance(): lax.all_gather(own_result, 'row', axis=0, tiled=True)]
    select_n x24, local copies, waits for them, and re-layouts: 1.3 us -> 14.6 us  [advance(): solution = jnp.where(valid, updated, solution)]
    while x12 -> x126, local copies, waits for them, and re-layouts: 0.64 us -> 12.6 us
    dot_general x6, matrix products: 28.7 us -> 17.2 us  [advance(): own_result = jnp.dot(own_inverse, full_residual, precision=highest)]
  transfers between devices with their start and end apart: 24 -> 60, of which waited for: 18 -> 54; matrix products, arithmetic and copies ran while one was open for 0% -> 2% of each run, Pallas kernels for 0% -> 0%
where the time goes in v1:
time: 749 us; the launch traced here: 748 us
  waiting for transfers between devices  550 us (73%)
  matrix products  85.6 us (11%)
  starting transfers between devices  54.8 us (7%)
  local copies, waits for them, and re-layouts  37 us (5%)
  between operations  13.4 us (2%)
    ppermute x42, waiting for transfers between devices, advance(): lax.ppermute(ring[-1], 'row', [(dev, (dev + 1) % 8) for dev in range(8)])  274 us
    all_gather x6, waiting for transfers between devices, advance(): lax.all_gather(own_result, 'row', axis=0, tiled=True)  249 us
    dot_general x6, matrix products, fold_update(): return carry + jnp.dot(panel_rows, piece, precision=highest)  68.4 us
    ppermute x12, starting transfers between devices, passed_along(): return lax.ppermute(block, axis, route)  49 us
    ppermute x12, waiting for transfers between devices, passed_along(): return lax.ppermute(block, axis, route)  28 us
    dot_general x6, matrix products, advance(): own_result = jnp.dot(own_inverse, full_residual, precision=highest)  17.2 us
  transfers between devices with their start and end apart: 60, of which 54 were waited for; matrix products, arithmetic and copies ran while one was open for 2% of the time, Pallas kernels for 0%

profile of v1, /device:TPU:1, one launch (start us, length us, event | category | flops | bytes accessed | tf_op | source)
XLA Modules:
  0.0 748.0 jit_solution(14993347390128350734)
XLA Ops:
  8.0 733.1 %while.19 = (s32[]{:T(128)}, f32[4,256,128]{1,0,2:T(4,128)S(1)}, f32[256,128]{0,1:T(8,128)}, f32[256,384]{1,0:T(8,128)}, s32[]{:T(128)}, /*index=5*/f32[1,256,38...) while((s32[]{:T(128)}, f32[4,256,128]{1,0,2:T(4,128)S(1)}, ...), condition=%wide.region_1.2_spmd, body=%wide.region_0.1_spmd.sunk | while | flops 4026728448 | bytes 41550776 | solution.py:63
  63.9 42.0 %all-gather.2.cloned.1.call-done = f32[2048,128]{0,1:T(8,128)} async-done(((f32[256,128]{0,1:T(8,128)}), f32[2048,128]{0,1:T(8,128)}) %all-gather.2.cloned.1.call-update) | async-done | bytes 1048592 | tf_op jit(solution)/shard_map/while/body/eval_jaxpr/all_gather | solution.py:50
  105.9 11.4 %fusion.13 = f32[1024,128]{0,1:T(8,128)S(1)} fusion(f32[1024,128]{0,1:T(8,128)S(1)} %bitcast.40, f32[2048,128]{0,1:T(8,128)} %all-gather.2.cloned.1.call-done, f32[1024,2048]{1,0:T(8,128)} %get-tuple-element.351), kind=kOutput, calls=%fused_computation.1.clone.1 | convolution fusion | flops 3221356544 | bytes 10485760 | tf_op jit(solution)/shard_map/while/body/eval_jaxpr/dot_general | solution.py:27
  146.4 7.2 collective-permute-done.2
  153.6 7.8 %collective-permute-done.3 = f32[256,128]{0,1:T(8,128)S(1)} collective-permute-done((f32[256,128]{0,1:T(8,128)S(1)}, f32[256,128]{0,1:T(8,128)S(1)}, u32[]{:S(2)}, u32[]{:S(2)}) %collective-permute-start.3) | collective-permute-done | bytes 131104 | tf_op jit(solution)/shard_map/while/body/eval_jaxpr/ppermute | solution.py:40
  186.6 41.3 %all-gather.2.cloned.1.call-done = f32[2048,128]{0,1:T(8,128)} async-done(((f32[256,128]{0,1:T(8,128)}), f32[2048,128]{0,1:T(8,128)}) %all-gather.2.cloned.1.call-update) | async-done | bytes 1048592 | tf_op jit(solution)/shard_map/while/body/eval_jaxpr/all_gather | solution.py:50
  227.9 11.4 %fusion.13 = f32[1024,128]{0,1:T(8,128)S(1)} fusion(f32[1024,128]{0,1:T(8,128)S(1)} %bitcast.40, f32[2048,128]{0,1:T(8,128)} %all-gather.2.cloned.1.call-done, f32[1024,2048]{1,0:T(8,128)} %get-tuple-element.351), kind=kOutput, calls=%fused_computation.1.clone.1 | convolution fusion | flops 3221356544 | bytes 10485760 | tf_op jit(solution)/shard_map/while/body/eval_jaxpr/dot_general | solution.py:27
  268.4 7.2 collective-permute-done.2
  275.6 7.8 %collective-permute-done.3 = f32[256,128]{0,1:T(8,128)S(1)} collective-permute-done((f32[256,128]{0,1:T(8,128)S(1)}, f32[256,128]{0,1:T(8,128)S(1)}, u32[]{:S(2)}, u32[]{:S(2)}) %collective-permute-start.3) | collective-permute-done | bytes 131104 | tf_op jit(solution)/shard_map/while/body/eval_jaxpr/ppermute | solution.py:40
  283.3 6.9 collective-permute-done.4
  308.5 41.3 %all-gather.2.cloned.1.call-done = f32[2048,128]{0,1:T(8,128)} async-done(((f32[256,128]{0,1:T(8,128)}), f32[2048,128]{0,1:T(8,128)}) %all-gather.2.cloned.1.call-update) | async-done | bytes 1048592 | tf_op jit(solution)/shard_map/while/body/eval_jaxpr/all_gather | solution.py:50
  349.8 11.4 %fusion.13 = f32[1024,128]{0,1:T(8,128)S(1)} fusion(f32[1024,128]{0,1:T(8,128)S(1)} %bitcast.40, f32[2048,128]{0,1:T(8,128)} %all-gather.2.cloned.1.call-done, f32[1024,2048]{1,0:T(8,128)} %get-tuple-element.351), kind=kOutput, calls=%fused_computation.1.clone.1 | convolution fusion | flops 3221356544 | bytes 10485760 | tf_op jit(solution)/shard_map/while/body/eval_jaxpr/dot_general | solution.py:27
  390.3 7.2 collective-permute-done.2
  397.5 7.8 %collective-permute-done.3 = f32[256,128]{0,1:T(8,128)S(1)} collective-permute-done((f32[256,128]{0,1:T(8,128)S(1)}, f32[256,128]{0,1:T(8,128)S(1)}, u32[]{:S(2)}, u32[]{:S(2)}) %collective-permute-start.3) | collective-permute-done | bytes 131104 | tf_op jit(solution)/shard_map/while/body/eval_jaxpr/ppermute | solution.py:40
  430.5 41.3 %all-gather.2.cloned.1.call-done = f32[2048,128]{0,1:T(8,128)} async-done(((f32[256,128]{0,1:T(8,128)}), f32[2048,128]{0,1:T(8,128)}) %all-gather.2.cloned.1.call-update) | async-done | bytes 1048592 | tf_op jit(solution)/shard_map/while/body/eval_jaxpr/all_gather | solution.py:50
  471.8 11.4 %fusion.13 = f32[1024,128]{0,1:T(8,128)S(1)} fusion(f32[1024,128]{0,1:T(8,128)S(1)} %bitcast.40, f32[2048,128]{0,1:T(8,128)} %all-gather.2.cloned.1.call-done, f32[1024,2048]{1,0:T(8,128)} %get-tuple-element.351), kind=kOutput, calls=%fused_computation.1.clone.1 | convolution fusion | flops 3221356544 | bytes 10485760 | tf_op jit(solution)/shard_map/while/body/eval_jaxpr/dot_general | solution.py:27
  512.3 7.2 collective-permute-done.2
  519.5 7.8 %collective-permute-done.3 = f32[256,128]{0,1:T(8,128)S(1)} collective-permute-done((f32[256,128]{0,1:T(8,128)S(1)}, f32[256,128]{0,1:T(8,128)S(1)}, u32[]{:S(2)}, u32[]{:S(2)}) %collective-permute-start.3) | collective-permute-done | bytes 131104 | tf_op jit(solution)/shard_map/while/body/eval_jaxpr/ppermute | solution.py:40
  552.4 41.3 %all-gather.2.cloned.1.call-done = f32[2048,128]{0,1:T(8,128)} async-done(((f32[256,128]{0,1:T(8,128)}), f32[2048,128]{0,1:T(8,128)}) %all-gather.2.cloned.1.call-update) | async-done | bytes 1048592 | tf_op jit(solution)/shard_map/while/body/eval_jaxpr/all_gather | solution.py:50
  593.8 11.4 %fusion.13 = f32[1024,128]{0,1:T(8,128)S(1)} fusion(f32[1024,128]{0,1:T(8,128)S(1)} %bitcast.40, f32[2048,128]{0,1:T(8,128)} %all-gather.2.cloned.1.call-done, f32[1024,2048]{1,0:T(8,128)} %get-tuple-element.351), kind=kOutput, calls=%fused_computation.1.clone.1 | convolution fusion | flops 3221356544 | bytes 10485760 | tf_op jit(solution)/shard_map/while/body/eval_jaxpr/dot_general | solution.py:27
  634.2 7.2 collective-permute-done.2
  641.5 7.8 %collective-permute-done.3 = f32[256,128]{0,1:T(8,128)S(1)} collective-permute-done((f32[256,128]{0,1:T(8,128)S(1)}, f32[256,128]{0,1:T(8,128)S(1)}, u32[]{:S(2)}, u32[]{:S(2)}) %collective-permute-start.3) | collective-permute-done | bytes 131104 | tf_op jit(solution)/shard_map/while/body/eval_jaxpr/ppermute | solution.py:40
  674.4 41.3 %all-gather.2.cloned.1.call-done = f32[2048,128]{0,1:T(8,128)} async-done(((f32[256,128]{0,1:T(8,128)}), f32[2048,128]{0,1:T(8,128)}) %all-gather.2.cloned.1.call-update) | async-done | bytes 1048592 | tf_op jit(solution)/shard_map/while/body/eval_jaxpr/all_gather | solution.py:50
  715.7 11.4 %fusion.13 = f32[1024,128]{0,1:T(8,128)S(1)} fusion(f32[1024,128]{0,1:T(8,128)S(1)} %bitcast.40, f32[2048,128]{0,1:T(8,128)} %all-gather.2.cloned.1.call-done, f32[1024,2048]{1,0:T(8,128)} %get-tuple-element.351), kind=kOutput, calls=%fused_computation.1.clone.1 | convolution fusion | flops 3221356544 | bytes 10485760 | tf_op jit(solution)/shard_map/while/body/eval_jaxpr/dot_general | solution.py:27
  (304 shorter events, 334.4 us)
Async XLA Ops:
  8.0 97.9 %all-gather.2.cloned.1.call-start = ((), (), s32[]{:S(2)}) async-start(), calls=%async_computation | async-start | bytes 1179648 | tf_op jit(solution)/shard_map/while/body/eval_jaxpr/all_gather | solution.py:50
  10.0 8.3 %collective-permute-start = (f32[256,128]{0,1:T(8,128)S(1)}, f32[256,128]{0,1:T(8,128)S(1)}, u32[]{:S(2)}, u32[]{:S(2)}) collective-permute-start(f32[256,128]{0,1:T(8,128)S(1)} %bitcast_subtract_fusion.2), channel_id=1, source_target_pairs={{0,1},{1,2},{2,3},{3,4},{4,5},{5,6},{6,7},{7,0},{8,9},{9,10},{10,1... | collective-permute-start | bytes 393224 | tf_op jit(solution)/shard_map/while/body/eval_jaxpr/ppermute | solution.py:40
  51.0 7.8 %collective-permute-start.6 = (f32[256,128]{0,1:T(8,128)S(1)}, f32[256,128]{0,1:T(8,128)}, u32[]{:S(2)}, u32[]{:S(2)}) collective-permute-start(f32[256,128]{0,1:T(8,128)S(1)} %collective-permute-done.5), channel_id=1, source_target_pairs={{0,1},{1,2},{2,3},{3,4},{4,5},{5,6},{6,7},{7,0},{8,9},{9,10},{10,1... | collective-permute-start | bytes 393224 | tf_op jit(solution)/shard_map/while/body/eval_jaxpr/ppermute | solution.py:40
  117.6 13.8 %collective-permute-start.7 = (f32[4,256,128]{1,0,2:T(4,128)S(1)}, f32[4,256,128]{1,0,2:T(4,128)S(1)}, u32[]{:S(2)}, u32[]{:S(2)}) collective-permute-start(f32[4,256,128]{1,0,2:T(4,128)S(1)} %reshape.31), channel_id=1, source_target_pairs={{0,8},{8,16},{16,24},{1,9},{9,17},{17,25},{2,10},{10,18},{18,26},{... | collective-permute-start | bytes 1572872 | tf_op jit(solution)/shard_map/while/body/eval_jaxpr/ppermute | solution.py:14
  124.0 7.4 collective-permute-start.8
  131.4 96.5 %all-gather.2.cloned.1.call-start = ((), (), s32[]{:S(2)}) async-start(), calls=%async_computation | async-start | bytes 1179648 | tf_op jit(solution)/shard_map/while/body/eval_jaxpr/all_gather | solution.py:50
  153.6 7.8 %collective-permute-start.3 = (f32[256,128]{0,1:T(8,128)S(1)}, f32[256,128]{0,1:T(8,128)S(1)}, u32[]{:S(2)}, u32[]{:S(2)}) collective-permute-start(f32[256,128]{0,1:T(8,128)S(1)} %collective-permute-done.2), channel_id=1, source_target_pairs={{0,1},{1,2},{2,3},{3,4},{4,5},{5,6},{6,7},{7,0},{8,9},{9,10},{10,1... | collective-permute-start | bytes 393224 | tf_op jit(solution)/shard_map/while/body/eval_jaxpr/ppermute | solution.py:40
  239.5 13.8 %collective-permute-start.7 = (f32[4,256,128]{1,0,2:T(4,128)S(1)}, f32[4,256,128]{1,0,2:T(4,128)S(1)}, u32[]{:S(2)}, u32[]{:S(2)}) collective-permute-start(f32[4,256,128]{1,0,2:T(4,128)S(1)} %reshape.31), channel_id=1, source_target_pairs={{0,8},{8,16},{16,24},{1,9},{9,17},{17,25},{2,10},{10,18},{18,26},{... | collective-permute-start | bytes 1572872 | tf_op jit(solution)/shard_map/while/body/eval_jaxpr/ppermute | solution.py:14
  246.0 7.4 collective-permute-start.8
  253.3 96.5 %all-gather.2.cloned.1.call-start = ((), (), s32[]{:S(2)}) async-start(), calls=%async_computation | async-start | bytes 1179648 | tf_op jit(solution)/shard_map/while/body/eval_jaxpr/all_gather | solution.py:50
  275.6 7.8 %collective-permute-start.3 = (f32[256,128]{0,1:T(8,128)S(1)}, f32[256,128]{0,1:T(8,128)S(1)}, u32[]{:S(2)}, u32[]{:S(2)}) collective-permute-start(f32[256,128]{0,1:T(8,128)S(1)} %collective-permute-done.2), channel_id=1, source_target_pairs={{0,1},{1,2},{2,3},{3,4},{4,5},{5,6},{6,7},{7,0},{8,9},{9,10},{10,1... | collective-permute-start | bytes 393224 | tf_op jit(solution)/shard_map/while/body/eval_jaxpr/ppermute | solution.py:40
  361.5 13.8 %collective-permute-start.7 = (f32[4,256,128]{1,0,2:T(4,128)S(1)}, f32[4,256,128]{1,0,2:T(4,128)S(1)}, u32[]{:S(2)}, u32[]{:S(2)}) collective-permute-start(f32[4,256,128]{1,0,2:T(4,128)S(1)} %reshape.31), channel_id=1, source_target_pairs={{0,8},{8,16},{16,24},{1,9},{9,17},{17,25},{2,10},{10,18},{18,26},{... | collective-permute-start | bytes 1572872 | tf_op jit(solution)/shard_map/while/body/eval_jaxpr/ppermute | solution.py:14
  367.9 7.4 collective-permute-start.8
  375.3 96.5 %all-gather.2.cloned.1.call-start = ((), (), s32[]{:S(2)}) async-start(), calls=%async_computation | async-start | bytes 1179648 | tf_op jit(solution)/shard_map/while/body/eval_jaxpr/all_gather | solution.py:50
  397.5 7.8 %collective-permute-start.3 = (f32[256,128]{0,1:T(8,128)S(1)}, f32[256,128]{0,1:T(8,128)S(1)}, u32[]{:S(2)}, u32[]{:S(2)}) collective-permute-start(f32[256,128]{0,1:T(8,128)S(1)} %collective-permute-done.2), channel_id=1, source_target_pairs={{0,1},{1,2},{2,3},{3,4},{4,5},{5,6},{6,7},{7,0},{8,9},{9,10},{10,1... | collective-permute-start | bytes 393224 | tf_op jit(solution)/shard_map/while/body/eval_jaxpr/ppermute | solution.py:40
  483.5 13.8 %collective-permute-start.7 = (f32[4,256,128]{1,0,2:T(4,128)S(1)}, f32[4,256,128]{1,0,2:T(4,128)S(1)}, u32[]{:S(2)}, u32[]{:S(2)}) collective-permute-start(f32[4,256,128]{1,0,2:T(4,128)S(1)} %reshape.31), channel_id=1, source_target_pairs={{0,8},{8,16},{16,24},{1,9},{9,17},{17,25},{2,10},{10,18},{18,26},{... | collective-permute-start | bytes 1572872 | tf_op jit(solution)/shard_map/while/body/eval_jaxpr/ppermute | solution.py:14
  489.9 7.4 collective-permute-start.8
  497.2 96.5 %all-gather.2.cloned.1.call-start = ((), (), s32[]{:S(2)}) async-start(), calls=%async_computation | async-start | bytes 1179648 | tf_op jit(solution)/shard_map/while/body/eval_jaxpr/all_gather | solution.py:50
  519.5 7.8 %collective-permute-start.3 = (f32[256,128]{0,1:T(8,128)S(1)}, f32[256,128]{0,1:T(8,128)S(1)}, u32[]{:S(2)}, u32[]{:S(2)}) collective-permute-start(f32[256,128]{0,1:T(8,128)S(1)} %collective-permute-done.2), channel_id=1, source_target_pairs={{0,1},{1,2},{2,3},{3,4},{4,5},{5,6},{6,7},{7,0},{8,9},{9,10},{10,1... | collective-permute-start | bytes 393224 | tf_op jit(solution)/shard_map/while/body/eval_jaxpr/ppermute | solution.py:40
  605.4 13.8 %collective-permute-start.7 = (f32[4,256,128]{1,0,2:T(4,128)S(1)}, f32[4,256,128]{1,0,2:T(4,128)S(1)}, u32[]{:S(2)}, u32[]{:S(2)}) collective-permute-start(f32[4,256,128]{1,0,2:T(4,128)S(1)} %reshape.31), channel_id=1, source_target_pairs={{0,8},{8,16},{16,24},{1,9},{9,17},{17,25},{2,10},{10,18},{18,26},{... | collective-permute-start | bytes 1572872 | tf_op jit(solution)/shard_map/while/body/eval_jaxpr/ppermute | solution.py:14
  611.8 7.4 collective-permute-start.8
  619.2 96.5 %all-gather.2.cloned.1.call-start = ((), (), s32[]{:S(2)}) async-start(), calls=%async_computation | async-start | bytes 1179648 | tf_op jit(solution)/shard_map/while/body/eval_jaxpr/all_gather | solution.py:50
  641.4 7.8 %collective-permute-start.3 = (f32[256,128]{0,1:T(8,128)S(1)}, f32[256,128]{0,1:T(8,128)S(1)}, u32[]{:S(2)}, u32[]{:S(2)}) collective-permute-start(f32[256,128]{0,1:T(8,128)S(1)} %collective-permute-done.2), channel_id=1, source_target_pairs={{0,1},{1,2},{2,3},{3,4},{4,5},{5,6},{6,7},{7,0},{8,9},{9,10},{10,1... | collective-permute-start | bytes 393224 | tf_op jit(solution)/shard_map/while/body/eval_jaxpr/ppermute | solution.py:40
  727.4 13.8 %collective-permute-start.7 = (f32[4,256,128]{1,0,2:T(4,128)S(1)}, f32[4,256,128]{1,0,2:T(4,128)S(1)}, u32[]{:S(2)}, u32[]{:S(2)}) collective-permute-start(f32[4,256,128]{1,0,2:T(4,128)S(1)} %reshape.31), channel_id=1, source_target_pairs={{0,8},{8,16},{16,24},{1,9},{9,17},{17,25},{2,10},{10,18},{18,26},{... | collective-permute-start | bytes 1572872 | tf_op jit(solution)/shard_map/while/body/eval_jaxpr/ppermute | solution.py:14
  (48 other events, 328.8 us)
Sparse Core Ops, SparseCore 0:
  63.9 41.9 all-gather.1
  186.6 41.2 all-gather.1
  308.5 41.2 all-gather.1
  430.5 41.2 all-gather.1
  552.5 41.2 all-gather.1
  674.4 41.2 all-gather.1
